TPU v7x, 128 devices: a whole 4x4x4 slice. The times are simulated.
128 devices in a mesh: row: 8 (over x_lo, y), col: 16 (over z, x_hi, core).
Axes of the slice: x: 4 (x_hi: 2, x_lo: 2; x = x_hi * 2 + x_lo), y: 4, z: 4, core: 2. Of those that a mesh axis runs over, the one named last changes fastest.
Arguments:
- features: bfloat16 [65536, 256], P(('col', 'row')), may hold values from -6 to 6
- weight: bfloat16 [256, 256], replicated, may hold values from -0.375 to 0.375
- tile_values: bfloat16 [65536, 128, 128], P(('row', 'col')), may hold values from -0.046875 to 0.046875
- tile_row: int32 [65536], P(('row', 'col')), may hold values from 0 to 63, as said below
- tile_col: int32 [65536], P(('row', 'col')), may hold values from 0 to 31, as said below
- tile_count: int32 [8, 16], P('row', 'col'), may hold values from 128 to 512, as said below
- cotangent: bfloat16 [65536, 256], P(('row', 'col')), may hold values from -6 to 6
Outputs:
- activated: bfloat16 [65536, 256], P(('row', 'col'))
- grad_features: bfloat16 [65536, 256], P(('col', 'row'))
- grad_weight: float32 [256, 256], replicated
Inputs may be any that keep to these rules, and one draw needn't show every extreme that they name: `tile_count`: 512 on at least one device in every draw. Within each device's slots the pairs (tile_row, tile_col) are distinct. Within each device's slots the pairs (tile_row, tile_col) are distinct.
All inputs are finite; a program needn't handle non-finite values.
Results may differ from a plain program's by a relative error of at most 0.024.
Values may be sent and summed in bfloat16 or wider, within the bound.
A program may use at most 128 MiB of HBM per device.

v0:
```python
import math
import jax
import jax.numpy as jnp
from jax import lax
from jax.sharding import PartitionSpec as P


def silu_slope(values):
    sigma = jax.nn.sigmoid(values)
    return sigma * (1.0 + values * (1.0 - sigma))


def tile_products(tile_values, fetch_index, place_index, live_mask, source, out_tiles, forward):
    slots = tile_values.shape[0]
    tile_size = tile_values.shape[1]
    hidden = source.shape[-1]
    source_tiles = source.shape[0]
    source_flat = source.reshape(source_tiles, tile_size * hidden)
    group_size = math.gcd(slots, 64)
    turn_count = slots // group_size
    source_ids = jnp.arange(source_tiles, dtype=jnp.int32)
    out_ids = jnp.arange(out_tiles, dtype=jnp.int32)

    def step(running, step_index):
        offset = step_index * group_size
        blocks = lax.dynamic_slice_in_dim(tile_values, offset, group_size, 0)
        take = lax.dynamic_slice_in_dim(fetch_index, offset, group_size, 0)
        place = lax.dynamic_slice_in_dim(place_index, offset, group_size, 0)
        live_part = lax.dynamic_slice_in_dim(live_mask, offset, group_size, 0)
        take_onehot = (take[:, None] == source_ids[None, :]).astype(jnp.bfloat16)
        fetched = jnp.dot(take_onehot, source_flat, preferred_element_type=jnp.float32)
        fetched = fetched.astype(jnp.bfloat16).reshape(group_size, tile_size, hidden)
        if forward:
            product = jnp.einsum(
                "sab,sbf->saf", blocks, fetched, preferred_element_type=jnp.float32
            )
        else:
            product = jnp.einsum(
                "sab,saf->sbf", blocks, fetched, preferred_element_type=jnp.float32
            )
        place_onehot = (place[:, None] == out_ids[None, :]).astype(jnp.float32) * live_part[:, None]
        added = lax.dot_general(
            place_onehot,
            product.reshape(group_size, tile_size * hidden),
            (((0,), (0,)), ((), ())),
            precision=lax.Precision.HIGHEST,
            preferred_element_type=jnp.float32,
        )
        return (running + added, None)

    start_value = jnp.zeros((out_tiles, tile_size * hidden), jnp.float32)
    result = lax.scan(step, start_value, jnp.arange(turn_count, dtype=jnp.int32))[0]
    return result.reshape(out_tiles * tile_size, hidden)


def body(features, weight, tile_values, tile_row, tile_col, tile_count, cotangent):
    row_count = lax.axis_size("row")
    col_count = lax.axis_size("col")
    node_dev = features.shape[0]
    hidden = features.shape[1]
    tile_size = tile_values.shape[1]
    slots = tile_values.shape[0]
    row_tiles = node_dev * col_count // tile_size
    col_tiles = node_dev * row_count // tile_size
    live_mask = (jnp.arange(slots, dtype=jnp.int32) < tile_count[0, 0]).astype(jnp.float32)
    projected = jnp.dot(features, weight, preferred_element_type=jnp.float32).astype(jnp.bfloat16)
    panel_rows = lax.all_gather(projected, "row", axis=0, tiled=True).reshape(
        col_tiles, tile_size, hidden
    )
    forward_part = tile_products(
        tile_values, tile_col, tile_row, live_mask, panel_rows, row_tiles, True
    )
    forward_part = forward_part.astype(jnp.bfloat16)
    summed = lax.psum_scatter(forward_part, "col", scatter_dimension=0, tiled=True).astype(
        jnp.float32
    )
    activated = jax.nn.silu(summed).astype(jnp.bfloat16)
    slope = (cotangent.astype(jnp.float32) * silu_slope(summed)).astype(jnp.bfloat16)
    slope_full = lax.all_gather(slope, "col", axis=0, tiled=True)
    slope_tiles = slope_full.reshape(row_tiles, tile_size, hidden)
    column_part = tile_products(
        tile_values, tile_row, tile_col, live_mask, slope_tiles, col_tiles, False
    )
    column_part = column_part.astype(jnp.bfloat16)
    grad_nodes = (
        lax.psum_scatter(column_part, "row", scatter_dimension=0, tiled=True)
        .astype(jnp.float32)
        .astype(jnp.bfloat16)
    )
    grad_features = lax.dot_general(
        grad_nodes, weight, (((1,), (1,)), ((), ())), preferred_element_type=jnp.float32
    ).astype(jnp.bfloat16)
    weight_term = lax.dot_general(
        features, grad_nodes, (((0,), (0,)), ((), ())), preferred_element_type=jnp.float32
    )
    grad_weight = lax.psum(weight_term, ("row", "col"))
    return (activated, grad_features, grad_weight)


def solution(mesh):
    placed = (
        P(("col", "row"), None),
        P(),
        P(("row", "col"), None, None),
        P(("row", "col")),
        P(("row", "col")),
        P("row", "col"),
        P(("row", "col"), None),
    )
    return jax.shard_map(
        body,
        mesh=mesh,
        in_specs=placed,
        out_specs=(P(("row", "col"), None), P(("col", "row"), None), P()),
        check_vma=False,
    )
```

profile of v0, /device:TPU:1, one launch (start us, length us, event | category | flops | bytes accessed | tf_op | source)
XLA Modules:
  0.0 843.4 jit_solution(16008225680619883002)
XLA Ops:
  10.7 39.1 %all-gather.3.cloned.1.call-done = bf16[4096,256]{1,0:T(8,128)(2,1)} async-done(((bf16[512,256]{1,0:T(8,128)(2,1)}), bf16[4096,256]{1,0:T(8,128)(2,1)}) %all-gather.3.cloned.1.call-update) | async-done | bytes 2097168 | tf_op jit(solution)/shard_map/all_gather | solution.py:67
  52.7 223.3 %while.22 = (s32[]{:T(128)}, f32[64,32768]{1,0:T(8,128)}, s32[8]{0:T(128)S(1)}, s32[512]{0:T(512)S(1)}, f32[512]{0:T(512)S(1)}, /*index=5*/bf16[512,128,128]{2,1...) while((s32[]{:T(128)}, f32[64,32768]{1,0:T(8,128)}, ...), condition=%wide.region_1.2_spmd.clone, body=%wide.region_0.1_spmd.clone.sunk | while | flops 2288003072 | bytes 71305672 | solution.py:52
  59.3 8.0 copy.22
  67.4 12.1 %convolution_add_fusion.4 = f32[64,32768]{1,0:T(8,128)} fusion(f32[64,32768]{1,0:T(8,128)} %bitcast.61, f32[64,32768]{1,0:T(8,128)} %get-tuple-element.327, pred[]{:T(512)S(6)} %compare.6, f32[64]{0:T(128)S(1)} %dynamic_slice.58, s32[64]{0:T(128)S(1)} %dynamic_slice.59), kind=kOutput, calls=%fused_computation.4.clone.1 | convolution fusion | flops 1614815232 | bytes 25166336 | tf_op jit(solution)/shard_map/while/body/eval_jaxpr/dot_general | solution.py:42
  86.1 8.0 copy.22
  94.2 13.4 %convolution_add_fusion.4 = f32[64,32768]{1,0:T(8,128)} fusion(f32[64,32768]{1,0:T(8,128)} %bitcast.61, f32[64,32768]{1,0:T(8,128)} %get-tuple-element.327, pred[]{:T(512)S(6)} %compare.6, f32[64]{0:T(128)S(1)} %dynamic_slice.58, s32[64]{0:T(128)S(1)} %dynamic_slice.59), kind=kOutput, calls=%fused_computation.4.clone.1 | convolution fusion | flops 1614815232 | bytes 25166336 | tf_op jit(solution)/shard_map/while/body/eval_jaxpr/dot_general | solution.py:42
  114.1 8.0 copy.22
  122.2 13.4 %convolution_add_fusion.4 = f32[64,32768]{1,0:T(8,128)} fusion(f32[64,32768]{1,0:T(8,128)} %bitcast.61, f32[64,32768]{1,0:T(8,128)} %get-tuple-element.327, pred[]{:T(512)S(6)} %compare.6, f32[64]{0:T(128)S(1)} %dynamic_slice.58, s32[64]{0:T(128)S(1)} %dynamic_slice.59), kind=kOutput, calls=%fused_computation.4.clone.1 | convolution fusion | flops 1614815232 | bytes 25166336 | tf_op jit(solution)/shard_map/while/body/eval_jaxpr/dot_general | solution.py:42
  142.2 8.0 copy.22
  150.3 13.4 %convolution_add_fusion.4 = f32[64,32768]{1,0:T(8,128)} fusion(f32[64,32768]{1,0:T(8,128)} %bitcast.61, f32[64,32768]{1,0:T(8,128)} %get-tuple-element.327, pred[]{:T(512)S(6)} %compare.6, f32[64]{0:T(128)S(1)} %dynamic_slice.58, s32[64]{0:T(128)S(1)} %dynamic_slice.59), kind=kOutput, calls=%fused_computation.4.clone.1 | convolution fusion | flops 1614815232 | bytes 25166336 | tf_op jit(solution)/shard_map/while/body/eval_jaxpr/dot_general | solution.py:42
  170.3 8.0 copy.22
  178.4 13.4 %convolution_add_fusion.4 = f32[64,32768]{1,0:T(8,128)} fusion(f32[64,32768]{1,0:T(8,128)} %bitcast.61, f32[64,32768]{1,0:T(8,128)} %get-tuple-element.327, pred[]{:T(512)S(6)} %compare.6, f32[64]{0:T(128)S(1)} %dynamic_slice.58, s32[64]{0:T(128)S(1)} %dynamic_slice.59), kind=kOutput, calls=%fused_computation.4.clone.1 | convolution fusion | flops 1614815232 | bytes 25166336 | tf_op jit(solution)/shard_map/while/body/eval_jaxpr/dot_general | solution.py:42
  198.3 8.0 copy.22
  206.4 13.4 %convolution_add_fusion.4 = f32[64,32768]{1,0:T(8,128)} fusion(f32[64,32768]{1,0:T(8,128)} %bitcast.61, f32[64,32768]{1,0:T(8,128)} %get-tuple-element.327, pred[]{:T(512)S(6)} %compare.6, f32[64]{0:T(128)S(1)} %dynamic_slice.58, s32[64]{0:T(128)S(1)} %dynamic_slice.59), kind=kOutput, calls=%fused_computation.4.clone.1 | convolution fusion | flops 1614815232 | bytes 25166336 | tf_op jit(solution)/shard_map/while/body/eval_jaxpr/dot_general | solution.py:42
  226.4 8.0 copy.22
  234.5 13.4 %convolution_add_fusion.4 = f32[64,32768]{1,0:T(8,128)} fusion(f32[64,32768]{1,0:T(8,128)} %bitcast.61, f32[64,32768]{1,0:T(8,128)} %get-tuple-element.327, pred[]{:T(512)S(6)} %compare.6, f32[64]{0:T(128)S(1)} %dynamic_slice.58, s32[64]{0:T(128)S(1)} %dynamic_slice.59), kind=kOutput, calls=%fused_computation.4.clone.1 | convolution fusion | flops 1614815232 | bytes 25166336 | tf_op jit(solution)/shard_map/while/body/eval_jaxpr/dot_general | solution.py:42
  254.5 8.0 copy.22
  262.6 13.4 %convolution_add_fusion.4 = f32[64,32768]{1,0:T(8,128)} fusion(f32[64,32768]{1,0:T(8,128)} %bitcast.61, f32[64,32768]{1,0:T(8,128)} %get-tuple-element.327, pred[]{:T(512)S(6)} %compare.6, f32[64]{0:T(128)S(1)} %dynamic_slice.58, s32[64]{0:T(128)S(1)} %dynamic_slice.59), kind=kOutput, calls=%fused_computation.4.clone.1 | convolution fusion | flops 1614815232 | bytes 25166336 | tf_op jit(solution)/shard_map/while/body/eval_jaxpr/dot_general | solution.py:42
  276.0 5.7 convert_element_type.47
  281.7 7.4 convert_element_type.48
  289.2 83.9 %reduce-scatter.3.cloned.1.call-done = bf16[512,256]{1,0:T(8,128)(2,1)} async-done(((bf16[8192,256]{1,0:T(8,128)(2,1)}), bf16[512,256]{1,0:T(8,128)(2,1)}) %reduce-scatter.3.cloned.1.call-update) | async-done | bytes 262160 | tf_op jit(solution)/shard_map/reduce_scatter | solution.py:74
  375.2 57.3 %all-gather.5.cloned.1.call-done = bf16[8192,256]{1,0:T(8,128)(2,1)} async-done(((bf16[512,256]{1,0:T(8,128)(2,1)}), bf16[8192,256]{1,0:T(8,128)(2,1)}) %all-gather.5.cloned.1.call-update) | async-done | bytes 4194320 | tf_op jit(solution)/shard_map/all_gather | solution.py:79
  432.5 7.4 reshape_reshape.7
  439.9 204.1 %while.23 = (s32[]{:T(128)}, f32[32,32768]{1,0:T(8,128)}, s32[8]{0:T(128)S(1)}, s32[512]{0:T(512)S(1)}, f32[512]{0:T(512)S(1)}, /*index=5*/bf16[512,128,128]{2,1...) while((s32[]{:T(128)}, f32[32,32768]{1,0:T(8,128)}, ...), condition=%wide.region_4.5_spmd.clone, body=%wide.region_3.4_spmd.clone.sunk | while | flops 1614815232 | bytes 65014216 | solution.py:52
  441.2 3.5 convolution_convert_fusion.7
  448.7 8.0 copy.24
  456.8 8.0 convolution_add_fusion.5
  466.1 3.5 convolution_convert_fusion.7
  473.6 8.0 copy.24
  481.7 8.7 %convolution_add_fusion.5 = f32[32,32768]{1,0:T(8,128)} fusion(f32[64,32768]{1,0:T(8,128)} %bitcast.58, f32[32,32768]{1,0:T(8,128)} %get-tuple-element.363, pred[]{:T(512)S(6)} %compare.7, f32[64]{0:T(128)S(1)} %dynamic_slice.63, s32[64]{0:T(128)S(1)} %dynamic_slice.64), kind=kOutput, calls=%fused_computation.18.clone.1 | convolution fusion | flops 807407616 | bytes 16777728 | tf_op jit(solution)/shard_map/while/body/eval_jaxpr/dot_general | solution.py:42
  499.2 8.0 copy.24
  507.3 8.7 %convolution_add_fusion.5 = f32[32,32768]{1,0:T(8,128)} fusion(f32[64,32768]{1,0:T(8,128)} %bitcast.58, f32[32,32768]{1,0:T(8,128)} %get-tuple-element.363, pred[]{:T(512)S(6)} %compare.7, f32[64]{0:T(128)S(1)} %dynamic_slice.63, s32[64]{0:T(128)S(1)} %dynamic_slice.64), kind=kOutput, calls=%fused_computation.18.clone.1 | convolution fusion | flops 807407616 | bytes 16777728 | tf_op jit(solution)/shard_map/while/body/eval_jaxpr/dot_general | solution.py:42
  517.3 3.5 convolution_convert_fusion.7
  524.8 8.0 copy.24
  532.9 8.7 %convolution_add_fusion.5 = f32[32,32768]{1,0:T(8,128)} fusion(f32[64,32768]{1,0:T(8,128)} %bitcast.58, f32[32,32768]{1,0:T(8,128)} %get-tuple-element.363, pred[]{:T(512)S(6)} %compare.7, f32[64]{0:T(128)S(1)} %dynamic_slice.63, s32[64]{0:T(128)S(1)} %dynamic_slice.64), kind=kOutput, calls=%fused_computation.18.clone.1 | convolution fusion | flops 807407616 | bytes 16777728 | tf_op jit(solution)/shard_map/while/body/eval_jaxpr/dot_general | solution.py:42
  550.4 8.0 copy.24
  558.5 8.7 %convolution_add_fusion.5 = f32[32,32768]{1,0:T(8,128)} fusion(f32[64,32768]{1,0:T(8,128)} %bitcast.58, f32[32,32768]{1,0:T(8,128)} %get-tuple-element.363, pred[]{:T(512)S(6)} %compare.7, f32[64]{0:T(128)S(1)} %dynamic_slice.63, s32[64]{0:T(128)S(1)} %dynamic_slice.64), kind=kOutput, calls=%fused_computation.18.clone.1 | convolution fusion | flops 807407616 | bytes 16777728 | tf_op jit(solution)/shard_map/while/body/eval_jaxpr/dot_general | solution.py:42
  568.5 3.5 convolution_convert_fusion.7
  576.0 8.0 copy.24
  584.1 8.7 %convolution_add_fusion.5 = f32[32,32768]{1,0:T(8,128)} fusion(f32[64,32768]{1,0:T(8,128)} %bitcast.58, f32[32,32768]{1,0:T(8,128)} %get-tuple-element.363, pred[]{:T(512)S(6)} %compare.7, f32[64]{0:T(128)S(1)} %dynamic_slice.63, s32[64]{0:T(128)S(1)} %dynamic_slice.64), kind=kOutput, calls=%fused_computation.18.clone.1 | convolution fusion | flops 807407616 | bytes 16777728 | tf_op jit(solution)/shard_map/while/body/eval_jaxpr/dot_general | solution.py:42
  594.1 3.5 convolution_convert_fusion.7
  601.6 8.0 copy.24
  609.7 8.7 %convolution_add_fusion.5 = f32[32,32768]{1,0:T(8,128)} fusion(f32[64,32768]{1,0:T(8,128)} %bitcast.58, f32[32,32768]{1,0:T(8,128)} %get-tuple-element.363, pred[]{:T(512)S(6)} %compare.7, f32[64]{0:T(128)S(1)} %dynamic_slice.63, s32[64]{0:T(128)S(1)} %dynamic_slice.64), kind=kOutput, calls=%fused_computation.18.clone.1 | convolution fusion | flops 807407616 | bytes 16777728 | tf_op jit(solution)/shard_map/while/body/eval_jaxpr/dot_general | solution.py:42
  619.7 3.5 convolution_convert_fusion.7
  627.2 8.0 copy.24
  635.3 8.7 %convolution_add_fusion.5 = f32[32,32768]{1,0:T(8,128)} fusion(f32[64,32768]{1,0:T(8,128)} %bitcast.58, f32[32,32768]{1,0:T(8,128)} %get-tuple-element.363, pred[]{:T(512)S(6)} %compare.7, f32[64]{0:T(128)S(1)} %dynamic_slice.63, s32[64]{0:T(128)S(1)} %dynamic_slice.64), kind=kOutput, calls=%fused_computation.18.clone.1 | convolution fusion | flops 807407616 | bytes 16777728 | tf_op jit(solution)/shard_map/while/body/eval_jaxpr/dot_general | solution.py:42
  648.8 35.1 %reduce-scatter.5.cloned.1.call-done = bf16[512,256]{1,0:T(8,128)(2,1)} async-done(((bf16[4096,256]{1,0:T(8,128)(2,1)}), bf16[512,256]{1,0:T(8,128)(2,1)}) %reduce-scatter.5.cloned.1.call-update) | async-done | bytes 262160 | tf_op jit(solution)/shard_map/reduce_scatter | solution.py:86
  687.8 147.3 %all-reduce.2.cloned.1.call-done = f32[256,256]{0,1:T(8,128)} async-done(((f32[256,256]{0,1:T(8,128)}), f32[256,256]{0,1:T(8,128)}) %all-reduce.2.cloned.1.call-update) | async-done | bytes 262160 | tf_op jit(solution)/shard_map/psum | solution.py:96
  (139 shorter events, 112.1 us)
Async XLA Ops:
  7.2 1.0 copy-start
  7.2 45.5 %copy-start.3 = (s32[512]{0:T(512)S(1)}, s32[512]{0:T(512)}, u32[]{:S(2)}) copy-start(s32[512]{0:T(512)} %param.14) | copy-start | bytes 6148
  7.2 45.5 %copy-start.4 = (s32[512]{0:T(512)S(1)}, s32[512]{0:T(512)}, u32[]{:S(2)}) copy-start(s32[512]{0:T(512)} %param.15) | copy-start | bytes 6148
  7.2 42.6 %all-gather.3.cloned.1.call-start = ((), (), s32[]{:S(2)}) async-start(), calls=%async_computation.2 | async-start | bytes 2359296 | tf_op jit(solution)/shard_map/all_gather | solution.py:67
  10.0 363.2 %reduce-scatter.3.cloned.1.call-start = ((), (), s32[]{:S(2)}) async-start(), calls=%async_computation.3 | async-start | bytes 4456448 | tf_op jit(solution)/shard_map/reduce_scatter | solution.py:74
  289.1 84.0 %copy-start.2 = (bf16[512,256]{1,0:T(8,128)(2,1)S(1)}, bf16[512,256]{1,0:T(8,128)(2,1)}, u32[]{:S(2)}) copy-start(bf16[512,256]{1,0:T(8,128)(2,1)} %param.17) | copy-start | bytes 786436
  289.2 143.4 %all-gather.5.cloned.1.call-start = ((), (), s32[]{:S(2)}) async-start(), calls=%async_computation.4 | async-start | bytes 4456448 | tf_op jit(solution)/shard_map/all_gather | solution.py:79
  375.2 308.7 %reduce-scatter.5.cloned.1.call-start = ((), (), s32[]{:S(2)}) async-start(), calls=%async_computation.5 | async-start | bytes 2359296 | tf_op jit(solution)/shard_map/reduce_scatter | solution.py:86
  646.4 39.5 %copy-start.1 = (bf16[256,256]{1,0:T(8,128)(2,1)S(1)}, bf16[256,256]{1,0:T(8,128)(2,1)}, u32[]{:S(2)}) copy-start(bf16[256,256]{1,0:T(8,128)(2,1)} %param.12) | copy-start | bytes 393220
  648.8 186.3 %all-reduce.2.cloned.1.call-start = ((), (), s32[]{:S(2)}) async-start(), calls=%async_computation.6 | async-start | bytes 524288 | tf_op jit(solution)/shard_map/psum | solution.py:96
Sparse Core Ops, SparseCore 0:
  10.3 39.4 all-gather.2
  289.3 83.8 reduce-scatter.2
  376.5 55.9 all-gather.4
  648.9 34.9 reduce-scatter.4
  689.8 145.2 all-reduce.1
where the time goes:
time: 845 us; the launch traced here: 843 us
  waiting for transfers between devices  363 us (43%)
  matrix products  264 us (31%)
  local copies, waits for them, and re-layouts  180 us (21%)
  between operations  14.5 us (2%)
  loops' own time  10.8 us (1%)
  other arithmetic  10.1 us (1%)
    dot_general x16, matrix products, step(): lax.dot_general(place_onehot, product.reshape(group_size, tile_size * hid...  175 us
    psum x1, waiting for transfers between devices, body(): grad_weight = lax.psum(weight_term, ('row', 'col'))  147 us
    while x32, local copies, waits for them, and re-layouts  145 us
    reduce_scatter x1, waiting for transfers between devices, body(): lax.psum_scatter(forward_part, 'col', scatter_dimension=0, tiled=True)  83.9 us
    all_gather x1, waiting for transfers between devices, body(): slope_full = lax.all_gather(slope, 'col', axis=0, tiled=True)  57.3 us
    all_gather x1, waiting for transfers between devices, body(): lax.all_gather(projected, 'row', axis=0, tiled=True)  39.1 us
    dot_general x16, matrix products, step(): jnp.dot(take_onehot, source_flat, preferred_element_type=jnp.float32)  38.1 us
    reduce_scatter x1, waiting for transfers between devices, body(): lax.psum_scatter(column_part, 'row', scatter_dimension=0, tiled=True)  35.1 us
  transfers between devices with their start and end apart: 5, of which 5 were waited for; matrix products, arithmetic and copies ran while one was open for 0% of the time, Pallas kernels for 0%

commit v1 on v0

--- a/solution.py
+++ b/solution.py
@@ -93,7 +93,7 @@
     weight_term = lax.dot_general(
         features, grad_nodes, (((0,), (0,)), ((), ())), preferred_element_type=jnp.float32
     )
-    grad_weight = lax.psum(weight_term, ("row", "col"))
+    grad_weight = lax.psum(lax.psum(weight_term, "col"), "row")
     return (activated, grad_features, grad_weight)
 
 

time: 845 us -> 915 us (1.083)
  waiting for transfers between devices: 363 us -> 428 us
    psum x1 -> x2, waiting for transfers between devices: 147 us -> 212 us  [body(): grad_weight = lax.psum(lax.psum(weight_term, 'col'), 'row')]
  transfers between devices with their start and end apart: 5 -> 6, of which waited for: 5 -> 6; matrix products, arithmetic and copies ran while one was open for 0% -> 0% of each run, Pallas kernels for 0% -> 0%
where the time goes in v1:
time: 915 us; the launch traced here: 909 us
  waiting for transfers between devices  428 us (47%)
  matrix products  264 us (29%)
  local copies, waits for them, and re-layouts  180 us (20%)
  between operations  14.9 us (2%)
  loops' own time  10.8 us (1%)
  other arithmetic  10.1 us (1%)
    psum x2, waiting for transfers between devices, body(): grad_weight = lax.psum(lax.psum(weight_term, 'col'), 'row')  212 us
    dot_general x16, matrix products, step(): lax.dot_general(place_onehot, product.reshape(group_size, tile_size * hid...  175 us
    while x32, local copies, waits for them, and re-layouts  145 us
    reduce_scatter x1, waiting for transfers between devices, body(): lax.psum_scatter(forward_part, 'col', scatter_dimension=0, tiled=True)  83.9 us
    all_gather x1, waiting for transfers between devices, body(): slope_full = lax.all_gather(slope, 'col', axis=0, tiled=True)  57.3 us
    all_gather x1, waiting for transfers between devices, body(): lax.all_gather(projected, 'row', axis=0, tiled=True)  39.1 us
    dot_general x16, matrix products, step(): jnp.dot(take_onehot, source_flat, preferred_element_type=jnp.float32)  38.1 us
    reduce_scatter x1, waiting for transfers between devices, body(): lax.psum_scatter(column_part, 'row', scatter_dimension=0, tiled=True)  35.1 us
  transfers between devices with their start and end apart: 6, of which 6 were waited for; matrix products, arithmetic and copies ran while one was open for 0% of the time, Pallas kernels for 0%

profile of v1, /device:TPU:1, one launch (start us, length us, event | category | flops | bytes accessed | tf_op | source)
XLA Modules:
  0.0 908.8 jit_solution(10860007074673705094)
XLA Ops:
  10.7 39.1 %all-gather.3.cloned.1.call-done = bf16[4096,256]{1,0:T(8,128)(2,1)} async-done(((bf16[512,256]{1,0:T(8,128)(2,1)}), bf16[4096,256]{1,0:T(8,128)(2,1)}) %all-gather.3.cloned.1.call-update) | async-done | bytes 2097168 | tf_op jit(solution)/shard_map/all_gather | solution.py:67
  52.7 223.3 %while.22 = (s32[]{:T(128)}, f32[64,32768]{1,0:T(8,128)}, s32[8]{0:T(128)S(1)}, s32[512]{0:T(512)S(1)}, f32[512]{0:T(512)S(1)}, /*index=5*/bf16[512,128,128]{2,1...) while((s32[]{:T(128)}, f32[64,32768]{1,0:T(8,128)}, ...), condition=%wide.region_1.2_spmd.clone, body=%wide.region_0.1_spmd.clone.sunk | while | flops 2288003072 | bytes 71305672 | solution.py:52
  59.3 8.0 copy.22
  67.4 12.1 %convolution_add_fusion.4 = f32[64,32768]{1,0:T(8,128)} fusion(f32[64,32768]{1,0:T(8,128)} %bitcast.61, f32[64,32768]{1,0:T(8,128)} %get-tuple-element.327, pred[]{:T(512)S(6)} %compare.6, f32[64]{0:T(128)S(1)} %dynamic_slice.58, s32[64]{0:T(128)S(1)} %dynamic_slice.59), kind=kOutput, calls=%fused_computation.4.clone.1 | convolution fusion | flops 1614815232 | bytes 25166336 | tf_op jit(solution)/shard_map/while/body/eval_jaxpr/dot_general | solution.py:42
  86.1 8.0 copy.22
  94.2 13.4 %convolution_add_fusion.4 = f32[64,32768]{1,0:T(8,128)} fusion(f32[64,32768]{1,0:T(8,128)} %bitcast.61, f32[64,32768]{1,0:T(8,128)} %get-tuple-element.327, pred[]{:T(512)S(6)} %compare.6, f32[64]{0:T(128)S(1)} %dynamic_slice.58, s32[64]{0:T(128)S(1)} %dynamic_slice.59), kind=kOutput, calls=%fused_computation.4.clone.1 | convolution fusion | flops 1614815232 | bytes 25166336 | tf_op jit(solution)/shard_map/while/body/eval_jaxpr/dot_general | solution.py:42
  114.1 8.0 copy.22
  122.2 13.4 %convolution_add_fusion.4 = f32[64,32768]{1,0:T(8,128)} fusion(f32[64,32768]{1,0:T(8,128)} %bitcast.61, f32[64,32768]{1,0:T(8,128)} %get-tuple-element.327, pred[]{:T(512)S(6)} %compare.6, f32[64]{0:T(128)S(1)} %dynamic_slice.58, s32[64]{0:T(128)S(1)} %dynamic_slice.59), kind=kOutput, calls=%fused_computation.4.clone.1 | convolution fusion | flops 1614815232 | bytes 25166336 | tf_op jit(solution)/shard_map/while/body/eval_jaxpr/dot_general | solution.py:42
  142.2 8.0 copy.22
  150.3 13.4 %convolution_add_fusion.4 = f32[64,32768]{1,0:T(8,128)} fusion(f32[64,32768]{1,0:T(8,128)} %bitcast.61, f32[64,32768]{1,0:T(8,128)} %get-tuple-element.327, pred[]{:T(512)S(6)} %compare.6, f32[64]{0:T(128)S(1)} %dynamic_slice.58, s32[64]{0:T(128)S(1)} %dynamic_slice.59), kind=kOutput, calls=%fused_computation.4.clone.1 | convolution fusion | flops 1614815232 | bytes 25166336 | tf_op jit(solution)/shard_map/while/body/eval_jaxpr/dot_general | solution.py:42
  170.3 8.0 copy.22
  178.4 13.4 %convolution_add_fusion.4 = f32[64,32768]{1,0:T(8,128)} fusion(f32[64,32768]{1,0:T(8,128)} %bitcast.61, f32[64,32768]{1,0:T(8,128)} %get-tuple-element.327, pred[]{:T(512)S(6)} %compare.6, f32[64]{0:T(128)S(1)} %dynamic_slice.58, s32[64]{0:T(128)S(1)} %dynamic_slice.59), kind=kOutput, calls=%fused_computation.4.clone.1 | convolution fusion | flops 1614815232 | bytes 25166336 | tf_op jit(solution)/shard_map/while/body/eval_jaxpr/dot_general | solution.py:42
  198.3 8.0 copy.22
  206.4 13.4 %convolution_add_fusion.4 = f32[64,32768]{1,0:T(8,128)} fusion(f32[64,32768]{1,0:T(8,128)} %bitcast.61, f32[64,32768]{1,0:T(8,128)} %get-tuple-element.327, pred[]{:T(512)S(6)} %compare.6, f32[64]{0:T(128)S(1)} %dynamic_slice.58, s32[64]{0:T(128)S(1)} %dynamic_slice.59), kind=kOutput, calls=%fused_computation.4.clone.1 | convolution fusion | flops 1614815232 | bytes 25166336 | tf_op jit(solution)/shard_map/while/body/eval_jaxpr/dot_general | solution.py:42
  226.4 8.0 copy.22
  234.5 13.4 %convolution_add_fusion.4 = f32[64,32768]{1,0:T(8,128)} fusion(f32[64,32768]{1,0:T(8,128)} %bitcast.61, f32[64,32768]{1,0:T(8,128)} %get-tuple-element.327, pred[]{:T(512)S(6)} %compare.6, f32[64]{0:T(128)S(1)} %dynamic_slice.58, s32[64]{0:T(128)S(1)} %dynamic_slice.59), kind=kOutput, calls=%fused_computation.4.clone.1 | convolution fusion | flops 1614815232 | bytes 25166336 | tf_op jit(solution)/shard_map/while/body/eval_jaxpr/dot_general | solution.py:42
  254.5 8.0 copy.22
  262.6 13.4 %convolution_add_fusion.4 = f32[64,32768]{1,0:T(8,128)} fusion(f32[64,32768]{1,0:T(8,128)} %bitcast.61, f32[64,32768]{1,0:T(8,128)} %get-tuple-element.327, pred[]{:T(512)S(6)} %compare.6, f32[64]{0:T(128)S(1)} %dynamic_slice.58, s32[64]{0:T(128)S(1)} %dynamic_slice.59), kind=kOutput, calls=%fused_computation.4.clone.1 | convolution fusion | flops 1614815232 | bytes 25166336 | tf_op jit(solution)/shard_map/while/body/eval_jaxpr/dot_general | solution.py:42
  276.0 5.7 convert_element_type.47
  281.7 7.4 convert_element_type.48
  289.2 83.9 %reduce-scatter.3.cloned.1.call-done = bf16[512,256]{1,0:T(8,128)(2,1)} async-done(((bf16[8192,256]{1,0:T(8,128)(2,1)}), bf16[512,256]{1,0:T(8,128)(2,1)}) %reduce-scatter.3.cloned.1.call-update) | async-done | bytes 262160 | tf_op jit(solution)/shard_map/reduce_scatter | solution.py:74
  375.2 57.3 %all-gather.5.cloned.1.call-done = bf16[8192,256]{1,0:T(8,128)(2,1)} async-done(((bf16[512,256]{1,0:T(8,128)(2,1)}), bf16[8192,256]{1,0:T(8,128)(2,1)}) %all-gather.5.cloned.1.call-update) | async-done | bytes 4194320 | tf_op jit(solution)/shard_map/all_gather | solution.py:79
  432.5 7.4 reshape_reshape.7
  439.9 204.1 %while.23 = (s32[]{:T(128)}, f32[32,32768]{1,0:T(8,128)}, s32[8]{0:T(128)S(1)}, s32[512]{0:T(512)S(1)}, f32[512]{0:T(512)S(1)}, /*index=5*/bf16[512,128,128]{2,1...) while((s32[]{:T(128)}, f32[32,32768]{1,0:T(8,128)}, ...), condition=%wide.region_4.5_spmd.clone, body=%wide.region_3.4_spmd.clone.sunk | while | flops 1614815232 | bytes 65014216 | solution.py:52
  441.2 3.5 convolution_convert_fusion.7
  448.7 8.0 copy.24
  456.8 8.0 convolution_add_fusion.5
  466.1 3.5 convolution_convert_fusion.7
  473.6 8.0 copy.24
  481.7 8.7 convolution_add_fusion.5
  499.2 8.0 copy.24
  507.3 8.7 convolution_add_fusion.5
  517.3 3.5 convolution_convert_fusion.7
  524.8 8.0 copy.24
  532.9 8.7 convolution_add_fusion.5
  550.4 8.0 copy.24
  558.5 8.7 convolution_add_fusion.5
  568.5 3.5 convolution_convert_fusion.7
  576.0 8.0 copy.24
  584.1 8.7 convolution_add_fusion.5
  601.6 8.0 copy.24
  609.7 8.7 convolution_add_fusion.5
  619.7 3.5 convolution_convert_fusion.7
  627.2 8.0 copy.24
  635.3 8.7 convolution_add_fusion.5
  648.8 35.1 %reduce-scatter.5.cloned.1.call-done = bf16[512,256]{1,0:T(8,128)(2,1)} async-done(((bf16[4096,256]{1,0:T(8,128)(2,1)}), bf16[512,256]{1,0:T(8,128)(2,1)}) %reduce-scatter.5.cloned.1.call-update) | async-done | bytes 262160 | tf_op jit(solution)/shard_map/reduce_scatter | solution.py:86
  685.9 142.0 %all-reduce.3.cloned.1.call-done = f32[256,256]{0,1:T(8,128)} async-done(((f32[256,256]{0,1:T(8,128)}), f32[256,256]{0,1:T(8,128)}) %all-reduce.3.cloned.1.call-update) | async-done | bytes 262160 | tf_op jit(solution)/shard_map/psum | solution.py:96
  829.9 70.3 %all-reduce.5.cloned.1.call-done = f32[256,256]{0,1:T(8,128)} async-done(((f32[256,256]{0,1:T(8,128)}), f32[256,256]{0,1:T(8,128)}) %all-reduce.5.cloned.1.call-update) | async-done | bytes 262160 | tf_op jit(solution)/shard_map/psum | solution.py:96
  (142 shorter events, 115.6 us)
Async XLA Ops:
  7.2 1.0 copy-start
  7.2 45.5 %copy-start.3 = (s32[512]{0:T(512)S(1)}, s32[512]{0:T(512)}, u32[]{:S(2)}) copy-start(s32[512]{0:T(512)} %param.14) | copy-start | bytes 6148
  7.2 45.5 %copy-start.4 = (s32[512]{0:T(512)S(1)}, s32[512]{0:T(512)}, u32[]{:S(2)}) copy-start(s32[512]{0:T(512)} %param.15) | copy-start | bytes 6148
  7.2 42.6 %all-gather.3.cloned.1.call-start = ((), (), s32[]{:S(2)}) async-start(), calls=%async_computation.2 | async-start | bytes 2359296 | tf_op jit(solution)/shard_map/all_gather | solution.py:67
  10.0 363.2 %reduce-scatter.3.cloned.1.call-start = ((), (), s32[]{:S(2)}) async-start(), calls=%async_computation.3 | async-start | bytes 4456448 | tf_op jit(solution)/shard_map/reduce_scatter | solution.py:74
  289.1 84.0 %copy-start.2 = (bf16[512,256]{1,0:T(8,128)(2,1)S(1)}, bf16[512,256]{1,0:T(8,128)(2,1)}, u32[]{:S(2)}) copy-start(bf16[512,256]{1,0:T(8,128)(2,1)} %param.17) | copy-start | bytes 786436
  289.2 143.4 %all-gather.5.cloned.1.call-start = ((), (), s32[]{:S(2)}) async-start(), calls=%async_computation.4 | async-start | bytes 4456448 | tf_op jit(solution)/shard_map/all_gather | solution.py:79
  375.2 308.7 %reduce-scatter.5.cloned.1.call-start = ((), (), s32[]{:S(2)}) async-start(), calls=%async_computation.5 | async-start | bytes 2359296 | tf_op jit(solution)/shard_map/reduce_scatter | solution.py:86
  646.4 181.6 %copy-start.1 = (bf16[256,256]{1,0:T(8,128)(2,1)S(1)}, bf16[256,256]{1,0:T(8,128)(2,1)}, u32[]{:S(2)}) copy-start(bf16[256,256]{1,0:T(8,128)(2,1)} %param.12) | copy-start | bytes 393220
  648.8 179.1 %all-reduce.3.cloned.1.call-start = ((), (), s32[]{:S(2)}) async-start(), calls=%async_computation.6 | async-start | bytes 524288 | tf_op jit(solution)/shard_map/psum | solution.py:96
  685.8 214.3 %all-reduce.5.cloned.1.call-start = ((), (), s32[]{:S(2)}) async-start(), calls=%async_computation.7 | async-start | bytes 524288 | tf_op jit(solution)/shard_map/psum | solution.py:96
Sparse Core Ops, SparseCore 0:
  10.3 39.4 all-gather.2
  289.3 83.8 reduce-scatter.2
  376.5 55.9 all-gather.4
  648.9 34.9 reduce-scatter.4
  686.9 140.9 all-reduce.2
  830.3 69.8 all-reduce.4
